TPU v7x, 32 devices: a whole 2x2x4 slice. The times are simulated.
32 devices in a mesh: expert: 8 (over z, x), fsdp: 4 (over y, core).
Axes of the slice: x: 2, y: 2, z: 4, core: 2. Of those that a mesh axis runs over, the one named last changes fastest.
Arguments:
- tokens: bfloat16 [160, 197, 512], P(('expert', 'fsdp')), may hold values from -6 to 6
- ln1_gain: bfloat16 [512], P('fsdp'), may hold values from 0.5 to 1.5
- ln1_bias: bfloat16 [512], P('fsdp'), may hold values from -1.796875 to 1.796875
- w_qkv: bfloat16 [512, 1536], P('fsdp'), may hold values from -0.25 to 0.25
- q_bias: bfloat16 [512], P('fsdp'), may hold values from -1.796875 to 1.796875
- v_bias: bfloat16 [512], P('fsdp'), may hold values from -1.796875 to 1.796875
- w_out: bfloat16 [512, 512], P('fsdp'), may hold values from -1.5 to 1.5
- out_bias: bfloat16 [512], P('fsdp'), may hold values from -1.796875 to 1.796875
- ln2_gain: bfloat16 [512], P('fsdp'), may hold values from 0.5 to 1.5
- ln2_bias: bfloat16 [512], P('fsdp'), may hold values from -1.796875 to 1.796875
- w_router: bfloat16 [512, 8], P('fsdp'), may hold values from -0.1875 to 0.1875
- expert_w1: bfloat16 [8, 512, 2048], P('expert', 'fsdp'), may hold values from -0.25 to 0.25
- expert_b1: bfloat16 [8, 2048], P('expert', 'fsdp'), may hold values from -1.796875 to 1.796875
- expert_w2: bfloat16 [8, 2048, 512], P('expert', 'fsdp'), may hold values from -0.75 to 0.75
- expert_b2: bfloat16 [8, 512], P('expert', 'fsdp'), may hold values from -6 to 6
- route_ids: int32 [31520, 2], P(('expert', 'fsdp')), may hold values from 0 to 7, all different within a row; in each aligned block of 985 rows (0 to 984, 985 to 1969, ...) at most 432 rows name the same one
- clip_threshold: int32 [8], replicated, may hold values from 2 to 4
- grad_output: bfloat16 [160, 197, 512], P(('expert', 'fsdp')), may hold values from -6 to 6
Outputs:
- output: bfloat16 [160, 197, 512], P(('expert', 'fsdp'))
- input_grad: float32 [160, 197, 512], P(('expert', 'fsdp'))
- grad_ln1_gain: float32 [512], P('fsdp')
- grad_ln1_bias: float32 [512], P('fsdp')
- grad_w_qkv: float32 [512, 1536], P('fsdp')
- grad_q_bias: float32 [512], P('fsdp')
- grad_v_bias: float32 [512], P('fsdp')
- grad_w_out: float32 [512, 512], P('fsdp')
- grad_out_bias: float32 [512], P('fsdp')
- grad_ln2_gain: float32 [512], P('fsdp')
- grad_ln2_bias: float32 [512], P('fsdp')
- grad_w_router: float32 [512, 8], P('fsdp')
- grad_expert_w1: float32 [8, 512, 2048], P('expert', 'fsdp')
- grad_expert_b1: float32 [8, 2048], P('expert', 'fsdp')
- grad_expert_w2: float32 [8, 2048, 512], P('expert', 'fsdp')
- grad_expert_b2: float32 [8, 512], P('expert', 'fsdp')
- clipped_qkv: bfloat16 [512, 1536], P('fsdp')
Inputs may be any that keep to these rules, and one draw needn't show every extreme that they name: `route_ids`: each row names 2 different experts; among the 985 rows of one device no expert is named by more than 432 rows, and in some device's rows one expert is named by exactly 432.
All inputs are finite; a program needn't handle non-finite values.
Results may differ from a plain program's by a relative error of at most 0.024.
Values may be sent and summed in bfloat16 or wider, within the bound.
No kernel may reach another device: no remote copies, remote signals or barrier semaphores. Data moves between devices by JAX's collectives and lax.ppermute only.
A program may use at most 256 MiB of HBM per device.

v0:
```python
import jax
import jax.numpy as jnp
from jax import lax
from jax.sharding import PartitionSpec as P

HEADS = 8
norm_eps = 1e-06
highest = lax.Precision.HIGHEST


def layer_norm(matrix, norm_gain, norm_shift):
    centred = matrix - jnp.mean(matrix, axis=1, keepdims=True)
    inverse = lax.rsqrt(jnp.mean(centred * centred, axis=1, keepdims=True) + norm_eps)
    normed = centred * inverse
    return (normed * norm_gain + norm_shift, normed, inverse)


def norm_backward(upstream, norm_gain, normed, inverse):
    scaled = upstream * norm_gain
    spread = (
        scaled
        - jnp.mean(scaled, axis=1, keepdims=True)
        - normed * jnp.mean(scaled * normed, axis=1, keepdims=True)
    )
    return (spread * inverse, jnp.sum(upstream * normed, axis=0), jnp.sum(upstream, axis=0))


def gelu_exact(values):
    return jax.nn.gelu(values, approximate=False)


def shards(
    tokens,
    ln1_gain,
    ln1_bias,
    w_qkv,
    q_bias,
    v_bias,
    w_out,
    out_bias,
    ln2_gain,
    ln2_bias,
    w_router,
    expert_w1,
    expert_b1,
    expert_w2,
    expert_b2,
    route_ids,
    clip_threshold,
    grad_output,
):
    gathered = (
        lax.all_gather(ln1_gain, "fsdp", axis=0, tiled=True),
        lax.all_gather(ln1_bias, "fsdp", axis=0, tiled=True),
        lax.all_gather(w_qkv, "fsdp", axis=0, tiled=True),
        lax.all_gather(q_bias, "fsdp", axis=0, tiled=True),
        lax.all_gather(v_bias, "fsdp", axis=0, tiled=True),
        lax.all_gather(w_out, "fsdp", axis=0, tiled=True),
        lax.all_gather(out_bias, "fsdp", axis=0, tiled=True),
        lax.all_gather(ln2_gain, "fsdp", axis=0, tiled=True),
        lax.all_gather(ln2_bias, "fsdp", axis=0, tiled=True),
        lax.all_gather(w_router, "fsdp", axis=0, tiled=True),
        lax.all_gather(expert_w1, "fsdp", axis=1, tiled=True),
        lax.all_gather(expert_b1, "fsdp", axis=1, tiled=True),
        lax.all_gather(expert_w2, "fsdp", axis=1, tiled=True),
        lax.all_gather(expert_b2, "fsdp", axis=1, tiled=True),
    )
    gain_one = gathered[0].astype(jnp.float32)
    shift_one = gathered[1].astype(jnp.float32)
    qkv_weight = gathered[2]
    query_bias = gathered[3].astype(jnp.float32)
    value_bias = gathered[4].astype(jnp.float32)
    out_weight = gathered[5]
    out_shift = gathered[6].astype(jnp.float32)
    gain_two = gathered[7].astype(jnp.float32)
    shift_two = gathered[8].astype(jnp.float32)
    router_weight = gathered[9].astype(jnp.float32)
    first_weight = gathered[10][0]
    first_bias = gathered[11][0].astype(jnp.float32)
    second_weight = gathered[12][0]
    second_bias = gathered[13][0].astype(jnp.float32)
    image_count, sequence, feature_width = tokens.shape
    token_count = image_count * sequence
    head_count = HEADS
    head_size = feature_width // head_count
    score_scale = head_size ** (-0.5)
    route_top = route_ids.shape[1]
    expert_total = router_weight.shape[1]
    capacity = (7 * token_count // (2 * expert_total) + 7) // 8 * 8
    head_shape = (image_count, sequence, head_count, head_size)
    residual = tokens.astype(jnp.float32).reshape(token_count, feature_width)
    normed_in, hat_one, inverse_one = layer_norm(residual, gain_one, shift_one)
    normed_low = normed_in.astype(jnp.bfloat16)
    projected = jnp.dot(normed_low, qkv_weight, preferred_element_type=jnp.float32)
    queries = (projected[:, :feature_width] + query_bias).astype(jnp.bfloat16).reshape(head_shape)
    key_rows = (
        projected[:, feature_width : 2 * feature_width].astype(jnp.bfloat16).reshape(head_shape)
    )
    value_rows = (
        (projected[:, 2 * feature_width :] + value_bias).astype(jnp.bfloat16).reshape(head_shape)
    )
    scores = (
        jnp.einsum("bqhd,bkhd->bhqk", queries, key_rows, preferred_element_type=jnp.float32)
        * score_scale
    )
    head_peak = jnp.max(scores, axis=(0, 2, 3))
    row_top = jnp.max(scores, axis=3, keepdims=True)
    log_total = row_top + jnp.log(jnp.sum(jnp.exp(scores - row_top), axis=3, keepdims=True))
    attn_low = jnp.exp(scores - log_total).astype(jnp.bfloat16)
    mixed_rows = jnp.einsum(
        "bhqk,bkhd->bqhd", attn_low, value_rows, preferred_element_type=jnp.float32
    )
    mixed_low = mixed_rows.astype(jnp.bfloat16).reshape(token_count, feature_width)
    hidden = (
        residual + jnp.dot(mixed_low, out_weight, preferred_element_type=jnp.float32) + out_shift
    )
    normed_mid, hat_two, inverse_two = layer_norm(hidden, gain_two, shift_two)
    route_prob = jax.nn.softmax(jnp.dot(normed_mid, router_weight, precision=highest), axis=1)
    picked = (
        route_ids[:, :, None] == lax.broadcasted_iota(jnp.int32, (1, 1, expert_total), 2)
    ).astype(jnp.int32)
    picked_float = picked.astype(jnp.float32)
    gate_values = jnp.sum(picked_float * route_prob[:, None, :], axis=2)
    picked_flat = picked.reshape(token_count * route_top, expert_total)
    slot_rank = jnp.sum(
        (jnp.cumsum(picked_flat, axis=0, dtype=jnp.int32) - picked_flat) * picked_flat,
        axis=1,
        dtype=jnp.int32,
    )
    slot_index = route_ids.reshape(-1) * capacity + slot_rank
    mid_low = normed_mid.astype(jnp.bfloat16)
    slot_rows = jnp.broadcast_to(
        mid_low[:, None, :], (token_count, route_top, feature_width)
    ).reshape(token_count * route_top, feature_width)
    outgoing = (
        jnp.zeros((expert_total * capacity, feature_width), jnp.bfloat16)
        .at[slot_index]
        .set(slot_rows)
        .reshape(expert_total, capacity, feature_width)
    )
    arrived = lax.all_to_all(outgoing, "expert", split_axis=0, concat_axis=0, tiled=True)
    flat_in = arrived.reshape(-1, feature_width)
    activation = gelu_exact(
        jnp.dot(flat_in, first_weight, preferred_element_type=jnp.float32) + first_bias
    ).astype(jnp.bfloat16)
    result = (
        jnp.dot(activation, second_weight, preferred_element_type=jnp.float32) + second_bias
    ).astype(jnp.bfloat16)
    produced = result.reshape(arrived.shape)
    returned = lax.all_to_all(produced, "expert", split_axis=0, concat_axis=0, tiled=True)
    slot_out = (
        returned.reshape(expert_total * capacity, feature_width)[slot_index]
        .astype(jnp.float32)
        .reshape(token_count, route_top, feature_width)
    )
    output = (
        (hidden + jnp.sum(gate_values[:, :, None] * slot_out, axis=1))
        .astype(jnp.bfloat16)
        .reshape(tokens.shape)
    )
    upstream = grad_output.astype(jnp.float32).reshape(token_count, feature_width)
    gate_grad = jnp.sum(slot_out * upstream[:, None, :], axis=2)
    slot_grad = (
        (gate_values[:, :, None] * upstream[:, None, :])
        .astype(jnp.bfloat16)
        .reshape(token_count * route_top, feature_width)
    )
    grad_buffer = (
        jnp.zeros((expert_total * capacity, feature_width), jnp.bfloat16)
        .at[slot_index]
        .set(slot_grad)
        .reshape(expert_total, capacity, feature_width)
    )
    grad_arrived = lax.all_to_all(grad_buffer, "expert", split_axis=0, concat_axis=0, tiled=True)
    flat_rows = arrived.reshape(-1, feature_width)
    flat_grad = grad_arrived.reshape(-1, feature_width)
    activation, gelu_back = jax.vjp(
        gelu_exact,
        jnp.dot(flat_rows, first_weight, preferred_element_type=jnp.float32) + first_bias,
    )
    act_low = activation.astype(jnp.bfloat16)
    grad_second = jnp.einsum("rh,rd->hd", act_low, flat_grad, preferred_element_type=jnp.float32)
    grad_second_bias = jnp.sum(flat_grad, axis=0, dtype=jnp.float32)
    act_grad = jnp.einsum("rd,hd->rh", flat_grad, second_weight, preferred_element_type=jnp.float32)
    pre_grad = gelu_back(act_grad)[0].astype(jnp.bfloat16)
    grad_first = jnp.einsum("rd,rh->dh", flat_rows, pre_grad, preferred_element_type=jnp.float32)
    grad_first_bias = jnp.sum(pre_grad, axis=0, dtype=jnp.float32)
    row_grad = (
        jnp.einsum("rh,dh->rd", pre_grad, first_weight, preferred_element_type=jnp.float32)
        .astype(jnp.bfloat16)
        .reshape(grad_arrived.shape)
    )
    row_back = lax.all_to_all(row_grad, "expert", split_axis=0, concat_axis=0, tiled=True)
    slot_back = (
        row_back.reshape(expert_total * capacity, feature_width)[slot_index]
        .astype(jnp.float32)
        .reshape(token_count, route_top, feature_width)
    )
    prob_grad = jnp.sum(picked_float * gate_grad[:, :, None], axis=1)
    logit_grad = route_prob * (prob_grad - jnp.sum(route_prob * prob_grad, axis=1, keepdims=True))
    mid_grad = jnp.sum(slot_back, axis=1) + jnp.einsum(
        "re,de->rd", logit_grad, router_weight, precision=highest
    )
    grad_router = jnp.einsum("rd,re->de", normed_mid, logit_grad, precision=highest)
    norm_part, grad_gain_two, grad_shift_two = norm_backward(
        mid_grad, gain_two, hat_two, inverse_two
    )
    hidden_grad = upstream + norm_part
    branch_low = hidden_grad.astype(jnp.bfloat16)
    grad_out_weight = jnp.einsum(
        "rd,re->de", mixed_low, branch_low, preferred_element_type=jnp.float32
    )
    grad_out_shift = jnp.sum(branch_low, axis=0, dtype=jnp.float32)
    mixed_grad = (
        jnp.einsum("re,de->rd", branch_low, out_weight, preferred_element_type=jnp.float32)
        .astype(jnp.bfloat16)
        .reshape(head_shape)
    )
    score_again = (
        jnp.einsum("bqhd,bkhd->bhqk", queries, key_rows, preferred_element_type=jnp.float32)
        * score_scale
    )
    attn_prob = jnp.exp(score_again - log_total)
    value_grad = jnp.einsum(
        "bhqk,bqhd->bkhd",
        attn_prob.astype(jnp.bfloat16),
        mixed_grad,
        preferred_element_type=jnp.float32,
    ).astype(jnp.bfloat16)
    weight_grad = jnp.einsum(
        "bqhd,bkhd->bhqk", mixed_grad, value_rows, preferred_element_type=jnp.float32
    )
    score_grad = (
        attn_prob * (weight_grad - jnp.sum(attn_prob * weight_grad, axis=3, keepdims=True))
    ).astype(jnp.bfloat16)
    query_grad = (
        jnp.einsum("bhqk,bkhd->bqhd", score_grad, key_rows, preferred_element_type=jnp.float32)
        * score_scale
    ).astype(jnp.bfloat16)
    key_grad = (
        jnp.einsum("bhqk,bqhd->bkhd", score_grad, queries, preferred_element_type=jnp.float32)
        * score_scale
    ).astype(jnp.bfloat16)
    qkv_grad = jnp.concatenate(
        [
            query_grad.reshape(token_count, feature_width),
            key_grad.reshape(token_count, feature_width),
            value_grad.reshape(token_count, feature_width),
        ],
        axis=1,
    )
    grad_qkv = jnp.einsum("rd,re->de", normed_low, qkv_grad, preferred_element_type=jnp.float32)
    grad_query_bias = jnp.sum(qkv_grad[:, :feature_width], axis=0, dtype=jnp.float32)
    grad_value_bias = jnp.sum(qkv_grad[:, 2 * feature_width :], axis=0, dtype=jnp.float32)
    in_grad = jnp.einsum("re,de->rd", qkv_grad, qkv_weight, preferred_element_type=jnp.float32)
    input_part, grad_gain_one, grad_shift_one = norm_backward(
        in_grad, gain_one, hat_one, inverse_one
    )
    input_grad = (hidden_grad + input_part).reshape(tokens.shape)
    shares = (
        lax.psum_scatter(
            grad_gain_one.astype(jnp.bfloat16), "fsdp", scatter_dimension=0, tiled=True
        ).astype(jnp.float32),
        lax.psum_scatter(
            grad_shift_one.astype(jnp.bfloat16), "fsdp", scatter_dimension=0, tiled=True
        ).astype(jnp.float32),
        lax.psum_scatter(
            grad_qkv.astype(jnp.bfloat16), "fsdp", scatter_dimension=0, tiled=True
        ).astype(jnp.float32),
        lax.psum_scatter(
            grad_query_bias.astype(jnp.bfloat16), "fsdp", scatter_dimension=0, tiled=True
        ).astype(jnp.float32),
        lax.psum_scatter(
            grad_value_bias.astype(jnp.bfloat16), "fsdp", scatter_dimension=0, tiled=True
        ).astype(jnp.float32),
        lax.psum_scatter(
            grad_out_weight.astype(jnp.bfloat16), "fsdp", scatter_dimension=0, tiled=True
        ).astype(jnp.float32),
        lax.psum_scatter(
            grad_out_shift.astype(jnp.bfloat16), "fsdp", scatter_dimension=0, tiled=True
        ).astype(jnp.float32),
        lax.psum_scatter(
            grad_gain_two.astype(jnp.bfloat16), "fsdp", scatter_dimension=0, tiled=True
        ).astype(jnp.float32),
        lax.psum_scatter(
            grad_shift_two.astype(jnp.bfloat16), "fsdp", scatter_dimension=0, tiled=True
        ).astype(jnp.float32),
        lax.psum_scatter(
            grad_router.astype(jnp.bfloat16), "fsdp", scatter_dimension=0, tiled=True
        ).astype(jnp.float32),
    )
    summed = (
        lax.psum(shares[0].astype(jnp.bfloat16), "expert").astype(jnp.float32),
        lax.psum(shares[1].astype(jnp.bfloat16), "expert").astype(jnp.float32),
        lax.psum(shares[2].astype(jnp.bfloat16), "expert").astype(jnp.float32),
        lax.psum(shares[3].astype(jnp.bfloat16), "expert").astype(jnp.float32),
        lax.psum(shares[4].astype(jnp.bfloat16), "expert").astype(jnp.float32),
        lax.psum(shares[5].astype(jnp.bfloat16), "expert").astype(jnp.float32),
        lax.psum(shares[6].astype(jnp.bfloat16), "expert").astype(jnp.float32),
        lax.psum(shares[7].astype(jnp.bfloat16), "expert").astype(jnp.float32),
        lax.psum(shares[8].astype(jnp.bfloat16), "expert").astype(jnp.float32),
        lax.psum(shares[9].astype(jnp.bfloat16), "expert").astype(jnp.float32),
    )
    expert_summed = (
        lax.psum_scatter(
            grad_first[None].astype(jnp.bfloat16), "fsdp", scatter_dimension=1, tiled=True
        ).astype(jnp.float32),
        lax.psum_scatter(
            grad_first_bias[None].astype(jnp.bfloat16), "fsdp", scatter_dimension=1, tiled=True
        ).astype(jnp.float32),
        lax.psum_scatter(
            grad_second[None].astype(jnp.bfloat16), "fsdp", scatter_dimension=1, tiled=True
        ).astype(jnp.float32),
        lax.psum_scatter(
            grad_second_bias[None].astype(jnp.bfloat16), "fsdp", scatter_dimension=1, tiled=True
        ).astype(jnp.float32),
    )
    peak_logit = lax.pmax(head_peak, ("expert", "fsdp"))
    limit_value = clip_threshold.astype(jnp.float32)
    root_factor = jnp.sqrt(limit_value / jnp.maximum(peak_logit, limit_value))
    column_scale = jnp.concatenate(
        [
            jnp.repeat(root_factor, head_size),
            jnp.repeat(root_factor, head_size),
            jnp.ones((feature_width,), jnp.float32),
        ]
    )
    clipped_qkv = (w_qkv.astype(jnp.float32) * column_scale).astype(jnp.bfloat16)
    return (
        output,
        input_grad,
        summed[0],
        summed[1],
        summed[2],
        summed[3],
        summed[4],
        summed[5],
        summed[6],
        summed[7],
        summed[8],
        summed[9],
        expert_summed[0],
        expert_summed[1],
        expert_summed[2],
        expert_summed[3],
        clipped_qkv,
    )


def solution(mesh):
    placed = (
        P(("expert", "fsdp"), None, None),
        P("fsdp"),
        P("fsdp"),
        P("fsdp", None),
        P("fsdp"),
        P("fsdp"),
        P("fsdp", None),
        P("fsdp"),
        P("fsdp"),
        P("fsdp"),
        P("fsdp", None),
        P("expert", "fsdp", None),
        P("expert", "fsdp"),
        P("expert", "fsdp", None),
        P("expert", "fsdp"),
        P(("expert", "fsdp"), None),
        P(),
        P(("expert", "fsdp"), None, None),
    )
    return jax.shard_map(
        shards,
        mesh=mesh,
        in_specs=placed,
        out_specs=(
            P(("expert", "fsdp"), None, None),
            P(("expert", "fsdp"), None, None),
            P("fsdp"),
            P("fsdp"),
            P("fsdp", None),
            P("fsdp"),
            P("fsdp"),
            P("fsdp", None),
            P("fsdp"),
            P("fsdp"),
            P("fsdp"),
            P("fsdp", None),
            P("expert", "fsdp", None),
            P("expert", "fsdp"),
            P("expert", "fsdp", None),
            P("expert", "fsdp"),
            P("fsdp", None),
        ),
        check_vma=False,
    )
```

profile of v0, /device:TPU:0, one launch (start us, length us, event | category | flops | bytes accessed | tf_op | source)
XLA Modules:
  0.0 718.8 jit_solution(18381751544721613083)
XLA Ops:
  11.8 6.0 all-gather
  17.8 5.3 all-gather.1
  23.1 5.0 all-gather.2
  28.2 5.0 all-gather.3
  33.2 5.0 all-gather.4
  38.2 5.0 all-gather.5
  43.3 5.0 all-gather.6
  52.3 7.9 %all_gather.47 = bf16[512,512]{1,0:T(8,128)(2,1)} all-gather(bf16[128,512]{1,0:T(8,128)(2,1)S(1)} %copy-done.46), channel_id=1, replica_groups=mesh['expert'=8,'fsdp'=4] {'fsdp'}, dimensions={0}, use_global_device_ids=true | all-gather | bytes 655360 | tf_op jit(solution)/shard_map/all_gather | solution.py:58
  85.4 5.5 fusion.26
  102.7 5.6 reshape.330
  108.3 13.3 %scatter_custom_fusion = bf16[3456,512]{1,0:T(8,128)(2,1)} fusion(s32[1970]{0:T(1024)S(1)} %bitcast.131, bf16[1970,512]{1,0:T(8,128)(2,1)} %reshape.330, bf16[]{:T(256)} %constant.17.clone.1), kind=kCustom, calls=%fused_computation.69 | custom fusion | bytes 3539456 | tf_op jit(solution)/shard_map/scatter | solution.py:138
  121.6 6.0 all-to-all-start
  130.6 4.8 mul.251
  135.5 6.1 mul.252
  141.6 5.2 all_gather.53
  146.8 5.0 all_gather.55
  152.4 5.6 all_gather.51
  161.2 18.5 %scatter_custom_fusion.1 = bf16[3456,512]{1,0:T(8,128)(2,1)} fusion(s32[1970]{0:T(1024)S(1)} %bitcast.132, f32[1970,512]{1,0:T(8,128)} %mul.252, f32[1970]{0:T(1024)S(1)} %mul.249, bf16[]{:T(256)} %constant.17.clone.1), kind=kCustom, calls=%fused_computation.63 | custom fusion | flops 2017280 | bytes 7581698 | tf_op jit(solution)/shard_map/scatter | solution.py:171
  179.8 27.6 %all-to-all-done = bf16[8,432,512]{2,1,0:T(8,128)(2,1)} async-done(((bf16[8,432,512]{2,1,0:T(8,128)(2,1)}), bf16[8,432,512]{2,1,0:T(8,128)(2,1)}, u32[]{:S(2)}, u32[]{:S(2)}) %all-to-all-start) | async-done | bytes 3538976 | tf_op jit(solution)/shard_map/all_to_all | solution.py:141
  207.3 4.7 all-to-all-start.2
  212.0 70.8 %multiply_convert_fusion = (bf16[3456,2048]{1,0:T(8,128)(2,1)}, f32[3456,2048]{1,0:T(8,128)}, f32[3456,2048]{1,0:T(8,128)}) fusion(f32[2048]{0:T(1024)S(1)} %bitcast.142, bf16[3456,512]{1,0:T(8,128)(2,1)} %bitcast.19, bf16[1,512,2048]{2,1,0:T(8,128)(2,1)} %all-gather.13.cloned.1.call-done), kind=kOutput, calls=%fused_computation.7 | convolution fusion | flops 7714897920 | bytes 76423168 | tf_op jit(solution)/shard_map/dot_general | solution.py:144
  282.8 12.5 %add_convert_fusion.1 = bf16[3456,512]{1,0:T(8,128)(2,1)} fusion(bf16[3456,2048]{1,0:T(8,128)(2,1)} %get-tuple-element.48, f32[512]{0:T(512)S(1)} %bitcast.144, bf16[1,2048,512]{2,1,0:T(8,128)(2,1)} %all-gather.15.cloned.1.call-done), kind=kOutput, calls=%fused_computation.25 | convolution fusion | flops 7251296256 | bytes 19793920 | tf_op jit(solution)/shard_map/dot_general | solution.py:147
  295.4 6.0 all-to-all-start.1
  305.0 31.9 %fusion.50 = (bf16[2048]{0:T(1024)(128)(2,1)S(1)}, bf16[3456,2048]{1,0:T(8,128)(2,1)}) fusion(f32[3456,2048]{1,0:T(8,128)} %get-tuple-element.49, bf16[3456,512]{1,0:T(8,128)(2,1)} %bitcast.27, bf16[1,2048,512]{2,1,0:T(8,128)(2,1)} %all-gather.15.cloned.1.call-done, f32[3456,2048]{1,0:T(8,128)} %get-tuple-element.57, f32[2048]{0:T(1024)S(1)} %bitcast.143), kind=kOutput, calls=%fused_computation.138 | convolution fusion | flops 7361001472 | bytes 76427264 | tf_op jit(solution)/shard_map/rd,hd->rh/dot_general | solution.py:184
  338.1 12.6 %convolution_convert_fusion = bf16[3456,512]{1,0:T(8,128)(2,1)} fusion(bf16[3456,2048]{1,0:T(8,128)(2,1)} %get-tuple-element.68, bf16[1,512,2048]{2,1,0:T(8,128)(2,1)} %all-gather.13.cloned.1.call-done), kind=kOutput, calls=%fused_computation.28 | convolution fusion | flops 7249526784 | bytes 19791872 | tf_op jit(solution)/shard_map/rh,dh->rd/dot_general | solution.py:189
  350.7 28.8 %all-to-all-done.1 = bf16[8,432,512]{2,1,0:T(8,128)(2,1)S(1)} async-done(((bf16[8,432,512]{2,1,0:T(8,128)(2,1)}), bf16[8,432,512]{2,1,0:T(8,128)(2,1)S(1)}, u32[]{:S(2)}, u32[]{:S(2)}) %all-to-all-start.1) | async-done | bytes 3538976 | tf_op jit(solution)/shard_map/all_to_all | solution.py:150
  379.6 4.5 all-to-all-start.3
  384.1 13.0 %fusion.7 = bf16[1,2048,512]{2,1,0:T(8,128)(2,1)} fusion(bf16[3456,2048]{1,0:T(8,128)(2,1)} %get-tuple-element.48, bf16[3456,512]{1,0:T(8,128)(2,1)} %bitcast.27), kind=kOutput, calls=%fused_computation.36 | convolution fusion | flops 7248805888 | bytes 19791872 | tf_op jit(solution)/shard_map/rh,rd->hd/dot_general | solution.py:182
  397.7 13.0 %fusion.8 = bf16[1,512,2048]{2,1,0:T(8,128)(2,1)} fusion(bf16[3456,512]{1,0:T(8,128)(2,1)} %bitcast.19, bf16[3456,2048]{1,0:T(8,128)(2,1)} %get-tuple-element.68), kind=kOutput, calls=%fused_computation.37 | convolution fusion | flops 7248805888 | bytes 19791872 | tf_op jit(solution)/shard_map/rd,rh->dh/dot_general | solution.py:186
  410.7 9.1 %gather_fusion = bf16[1970,512]{1,0:T(8,128)(2,1)} fusion(bf16[3456,512]{1,0:T(8,128)(2,1)S(1)} %bitcast.112, s32[2048]{0:T(1024)S(1)} %pad_clamp_fusion), kind=kCustom, calls=%fused_computation | custom fusion | bytes 4042440 | tf_op jit(solution)/shard_map/gather | solution.py:152
  419.9 5.6 reshape.306
  425.5 13.6 %multiply_reduce_fusion.3 = (f32[985,2]{1,0:T(8,128)S(1)}, f32[985,512]{1,0:T(8,128)}) fusion(f32[985,2,512]{2,1,0:T(2,128)} %reshape.306, f32[985,512]{1,0:T(8,128)S(1)} %copy-done.7, f32[985,2]{1,0:T(8,128)S(1)} %copy-done.23), kind=kLoop, calls=%fused_computation.31 | loop fusion | flops 3528270 | bytes 8084880 | tf_op jit(solution)/shard_map/reduce_sum | solution.py:162
  439.4 23.3 %all-to-all-done.3 = bf16[8,432,512]{2,1,0:T(8,128)(2,1)} async-done(((bf16[8,432,512]{2,1,0:T(8,128)(2,1)}), bf16[8,432,512]{2,1,0:T(8,128)(2,1)}, u32[]{:S(2)}, u32[]{:S(2)}) %all-to-all-start.3) | async-done | bytes 3538976 | tf_op jit(solution)/shard_map/all_to_all | solution.py:193
  462.7 10.4 %gather_fusion.1 = bf16[1970,512]{1,0:T(8,128)(2,1)S(1)} fusion(bf16[3456,512]{1,0:T(8,128)(2,1)} %bitcast.29, s32[2048]{0:T(1024)S(1)} %pad_clamp_fusion), kind=kCustom, calls=%fused_computation.1 | custom fusion | bytes 4042440 | tf_op jit(solution)/shard_map/gather | solution.py:195
  473.1 4.7 reshape.309
  477.8 8.4 %reduce_sum.274 = f32[985,512]{1,0:T(8,128)} reduce(f32[985,2,512]{2,1,0:T(2,128)} %reshape.309, f32[]{:T(128)} %constant.40.clone.1), dimensions={1}, to_apply=%region_15.16 | reduce | flops 504320 | bytes 6051844 | tf_op jit(solution)/shard_map/reduce_sum | solution.py:201
  486.3 4.2 multiply_reduce_fusion.6
  495.9 4.2 copy.119
  503.6 6.7 multiply_reduce_fusion.1
  510.3 4.7 multiply_convert_fusion.1
  520.6 4.3 fusion.48
  524.8 4.1 copy.129
  563.9 38.0 %pmax.7 = f32[8]{0:T(128)S(1)} all-reduce(f32[8]{0:T(128)S(1)} %get-tuple-element.17), channel_id=1, replica_groups=mesh['expert'=8,'fsdp'=4] {'expert','fsdp'}, use_global_device_ids=true, to_apply=%region_58.59 | all-reduce | flops 8 | bytes 64 | tf_op jit(solution)/shard_map/pmax | solution.py:318
  604.4 6.5 multiply_reduce_fusion.7
  615.1 6.4 all-reduce.10
  627.2 4.5 reduce-scatter.22.cloned.1.call-done
  632.5 21.7 %all-reduce.8 = (bf16[128]{0:T(256)(128)(2,1)S(1)}, bf16[128]{0:T(256)(128)(2,1)S(1)}, bf16[128]{0:T(256)(128)(2,1)S(1)}, bf16[128]{0:T(256)(128)(2,1)S(1)}, bf1...) all-reduce(bf16[128]{0:T(256)(128)(2,1)S(1)} %dynamic-slice.1, ...), channel_id=1, replica_groups=mesh['expert'=8,'fsdp'=4] {'expert'}, use_global_device_ids=true, to_apply=%region_26.27 | all-reduce | flops 1920 | bytes 7680 | tf_op jit(solution)/shard_map/psum | solution.py:293
  658.4 49.8 %all-reduce.13.cloned.1.call-done = (bf16[128,1536]{1,0:T(8,128)(2,1)}, bf16[128,512]{1,0:T(8,128)(2,1)}) async-done(((bf16[128,1536]{1,0:T(8,128)(2,1)}, bf16[128,512]{1,0:T(8,128)(2,1)}), (bf16[128,1536]{1,0:T(8,128)(2,1)}, bf16[128,512]{1,0:T(8,128)(2,1)})) %all-reduce.13.cloned.1.call-update) | async-done | bytes 524304 | tf_op jit(solution)/shard_map/psum | solution.py:295
  (310 shorter events, 127.0 us)
Async XLA Ops:
  7.2 10.6 %copy-start.67 = (bf16[128]{0:T(256)(128)(2,1)S(1)}, bf16[128]{0:T(256)(128)(2,1)}, u32[]{:S(2)}) copy-start(bf16[128]{0:T(256)(128)(2,1)} %param.20) | copy-start | bytes 772
  7.2 15.9 %copy-start.68 = (bf16[128]{0:T(256)(128)(2,1)S(1)}, bf16[128]{0:T(256)(128)(2,1)}, u32[]{:S(2)}) copy-start(bf16[128]{0:T(256)(128)(2,1)} %param.23) | copy-start | bytes 772
  7.2 20.9 %copy-start.69 = (bf16[128]{0:T(256)(128)(2,1)S(1)}, bf16[128]{0:T(256)(128)(2,1)}, u32[]{:S(2)}) copy-start(bf16[128]{0:T(256)(128)(2,1)} %param.22) | copy-start | bytes 772
  7.2 25.9 %copy-start.70 = (bf16[128]{0:T(256)(128)(2,1)S(1)}, bf16[128]{0:T(256)(128)(2,1)}, u32[]{:S(2)}) copy-start(bf16[128]{0:T(256)(128)(2,1)} %param.25) | copy-start | bytes 772
  7.3 31.0 %copy-start.71 = (bf16[128]{0:T(256)(128)(2,1)S(1)}, bf16[128]{0:T(256)(128)(2,1)}, u32[]{:S(2)}) copy-start(bf16[128]{0:T(256)(128)(2,1)} %param.26) | copy-start | bytes 772
  7.3 36.0 %copy-start.72 = (bf16[128]{0:T(256)(128)(2,1)S(1)}, bf16[128]{0:T(256)(128)(2,1)}, u32[]{:S(2)}) copy-start(bf16[128]{0:T(256)(128)(2,1)} %param.27) | copy-start | bytes 772
  7.3 41.0 %copy-start.44 = (s32[985,2]{0,1:T(2,128)S(1)}, s32[985,2]{0,1:T(2,128)}, u32[]{:S(2)}) copy-start(s32[985,2]{0,1:T(2,128)} %param.33) | copy-start | bytes 23644
  7.3 53.0 %all-gather.11.cloned.1.call-start = ((), (), s32[]{:S(2)}) async-start(), calls=%async_computation.11 | async-start | bytes 1966080 | tf_op jit(solution)/shard_map/all_gather | solution.py:55
  9.5 42.8 %copy-start.46 = (bf16[128,512]{1,0:T(8,128)(2,1)S(1)}, bf16[128,512]{1,0:T(8,128)(2,1)}, u32[]{:S(2)}) copy-start(bf16[128,512]{1,0:T(8,128)(2,1)} %param.24) | copy-start | bytes 393220
  11.0 52.5 %copy-start.4 = (f32[985,512]{1,0:T(8,128)}, f32[985,512]{1,0:T(8,128)S(1)}, u32[]{:S(2)}) copy-start(f32[985,512]{1,0:T(8,128)S(1)} %reshape.278) | copy-start | bytes 6051844
  11.1 52.4 %copy-start.40 = (f32[985]{0:T(1024)}, f32[985]{0:T(1024)S(1)}, u32[]{:S(2)}) copy-start(f32[985]{0:T(1024)S(1)} %div.38) | copy-start | bytes 11824
  11.8 51.7 %copy-start.42 = (f32[985]{0:T(1024)}, f32[985]{0:T(1024)S(1)}, u32[]{:S(2)}) copy-start(f32[985]{0:T(1024)S(1)} %rsqrt.20) | copy-start | bytes 11824
  17.8 45.7 %copy-start.47 = (f32[4,1,128]{2,1,0:T(1,128)}, f32[4,1,128]{2,1,0:T(1,128)S(1)}, u32[]{:S(2)}) copy-start(f32[4,1,128]{2,1,0:T(1,128)S(1)} %convert_element_type.334) | copy-start | bytes 6148
  23.1 40.4 %copy-start.55 = (f32[4,1,128]{2,1,0:T(1,128)}, f32[4,1,128]{2,1,0:T(1,128)S(1)}, u32[]{:S(2)}) copy-start(f32[4,1,128]{2,1,0:T(1,128)S(1)} %convert_element_type.335) | copy-start | bytes 6148
  43.3 114.8 %copy-start.51 = (f32[4,1,128]{2,1,0:T(1,128)}, f32[4,1,128]{2,1,0:T(1,128)S(1)}, u32[]{:S(2)}) copy-start(f32[4,1,128]{2,1,0:T(1,128)S(1)} %convert_element_type.339) | copy-start | bytes 6148
  48.3 109.7 %copy-start.61 = (f32[4,1,128]{2,1,0:T(1,128)}, f32[4,1,128]{2,1,0:T(1,128)S(1)}, u32[]{:S(2)}) copy-start(f32[4,1,128]{2,1,0:T(1,128)S(1)} %convert_element_type.340) | copy-start | bytes 6148
  60.2 101.0 %copy-start.59 = (s32[1970,1]{0,1:T(1,128)}, s32[1970,1]{0,1:T(1,128)S(1)}, u32[]{:S(2)}) copy-start(s32[1970,1]{0,1:T(1,128)S(1)} %compare_select_fusion) | copy-start | bytes 23644
  99.6 58.5 %copy-start.1 = (f32[985,512]{1,0:T(8,128)}, f32[985,512]{1,0:T(8,128)S(1)}, u32[]{:S(2)}) copy-start(f32[985,512]{1,0:T(8,128)S(1)} %get-tuple-element.56) | copy-start | bytes 6051844
  99.6 58.5 %copy-start.36 = (f32[985]{0:T(1024)}, f32[985]{0:T(1024)S(1)}, u32[]{:S(2)}) copy-start(f32[985]{0:T(1024)S(1)} %broadcast_multiply_fusion.6) | copy-start | bytes 11824
  100.0 58.0 %copy-start.38 = (f32[985]{0:T(1024)}, f32[985]{0:T(1024)S(1)}, u32[]{:S(2)}) copy-start(f32[985]{0:T(1024)S(1)} %add_rsqrt_fusion.1) | copy-start | bytes 11824
  121.6 85.7 %all-to-all-start = ((bf16[8,432,512]{2,1,0:T(8,128)(2,1)}), bf16[8,432,512]{2,1,0:T(8,128)(2,1)}, u32[]{:S(2)}, u32[]{:S(2)}) async-start(bf16[8,432,512]{2,1,0:T(8,128)(2,1)} %bitcast.113), calls=%async_computation | async-start | bytes 7077888 | tf_op jit(solution)/shard_map/all_to_all | solution.py:141
  127.6 84.4 %all-gather.13.cloned.1.call-start = ((), (), s32[]{:S(2)}) async-start(), calls=%async_computation.12 | async-start | bytes 2621440 | tf_op jit(solution)/shard_map/all_gather | solution.py:63
  128.3 154.5 %all-gather.15.cloned.1.call-start = ((), (), s32[]{:S(2)}) async-start(), calls=%async_computation.13 | async-start | bytes 2621440 | tf_op jit(solution)/shard_map/all_gather | solution.py:65
  135.4 11.3 %copy-start.73 = (bf16[1,128]{1,0:T(2,128)(2,1)S(1)}, bf16[1,128]{1,0:T(2,128)(2,1)}, u32[]{:S(2)}) copy-start(bf16[1,128]{1,0:T(2,128)(2,1)} %param.32) | copy-start | bytes 772
  135.5 17.0 %copy-start.64 = (bf16[128,8]{0,1:T(8,128)(2,1)S(1)}, bf16[128,8]{0,1:T(8,128)(2,1)}, u32[]{:S(2)}) copy-start(bf16[128,8]{0,1:T(8,128)(2,1)} %param.28) | copy-start | bytes 6148
  158.0 21.7 %copy-start.49 = (bf16[512,8]{0,1:T(8,128)(2,1)}, bf16[512,8]{0,1:T(8,128)(2,1)S(1)}, u32[]{:S(2)}) copy-start(bf16[512,8]{0,1:T(8,128)(2,1)S(1)} %all_gather.51) | copy-start | bytes 24580
  159.5 20.3 %copy-start.53 = (f32[985]{0:T(1024)}, f32[985]{0:T(1024)S(1)}, u32[]{:S(2)}) copy-start(f32[985]{0:T(1024)S(1)} %get-tuple-element.58) | copy-start | bytes 11824
  159.5 20.2 %copy-start.57 = (f32[985]{0:T(1024)}, f32[985]{0:T(1024)S(1)}, u32[]{:S(2)}) copy-start(f32[985]{0:T(1024)S(1)} %fusion.38) | copy-start | bytes 11824
  160.9 18.8 %copy-start.22 = (f32[985,2]{1,0:T(8,128)}, f32[985,2]{1,0:T(8,128)S(1)}, u32[]{:S(2)}) copy-start(f32[985,2]{1,0:T(8,128)S(1)} %copy.114) | copy-start | bytes 23644
  207.3 88.1 %all-to-all-start.2 = ((bf16[8,432,512]{2,1,0:T(8,128)(2,1)}), bf16[8,432,512]{2,1,0:T(8,128)(2,1)}, u32[]{:S(2)}, u32[]{:S(2)}) async-start(bf16[8,432,512]{2,1,0:T(8,128)(2,1)} %bitcast.26), calls=%async_computation.2 | async-start | bytes 7077888 | tf_op jit(solution)/shard_map/all_to_all | solution.py:174
  212.0 70.8 %copy-start.65 = (f32[1,512]{1,0:T(1,128)S(1)}, f32[1,512]{1,0:T(1,128)}, u32[]{:S(2)}) copy-start(f32[1,512]{1,0:T(1,128)} %add.210) | copy-start | bytes 6148
  295.4 84.2 %all-to-all-start.1 = ((bf16[8,432,512]{2,1,0:T(8,128)(2,1)}), bf16[8,432,512]{2,1,0:T(8,128)(2,1)S(1)}, u32[]{:S(2)}, u32[]{:S(2)}) async-start(bf16[8,432,512]{2,1,0:T(8,128)(2,1)} %bitcast.115), calls=%async_computation.1 | async-start | bytes 7077888 | tf_op jit(solution)/shard_map/all_to_all | solution.py:150
  301.4 255.3 %reduce-scatter.26.cloned.1.call-start = ((), (), s32[]{:S(2)}) async-start(), calls=%async_computation.20 | async-start | bytes 163840
  304.8 253.3 %reduce-scatter.24.cloned.1.call-start = ((), (), s32[]{:S(2)}) async-start(), calls=%async_computation.19 | async-start | bytes 655360
  379.6 83.1 %all-to-all-start.3 = ((bf16[8,432,512]{2,1,0:T(8,128)(2,1)}), bf16[8,432,512]{2,1,0:T(8,128)(2,1)}, u32[]{:S(2)}, u32[]{:S(2)}) async-start(bf16[8,432,512]{2,1,0:T(8,128)(2,1)} %bitcast.114), calls=%async_computation.3 | async-start | bytes 7077888 | tf_op jit(solution)/shard_map/all_to_all | solution.py:193
  384.1 13.6 %copy-start.60 = (s32[1970,1]{0,1:T(1,128)S(1)}, s32[1970,1]{0,1:T(1,128)}, u32[]{:S(2)}) copy-start(s32[1970,1]{0,1:T(1,128)} %copy-done.59) | copy-start | bytes 23644
  384.1 175.5 %reduce-scatter.20.cloned.1.call-start = ((), (), s32[]{:S(2)}) async-start(), calls=%async_computation.17 | async-start | bytes 2621440 | tf_op jit(solution)/shard_map/reduce_scatter | solution.py:311
  397.2 164.6 %reduce-scatter.18.cloned.1.call-start = ((), (), s32[]{:S(2)}) async-start(), calls=%async_computation.16 | async-start | bytes 2621440 | tf_op jit(solution)/shard_map/reduce_scatter | solution.py:305
  410.7 204.2 %reduce-scatter.16.cloned.1.call-start = ((), (), s32[]{:S(2)}) async-start(), calls=%async_computation.15 | async-start | bytes 655360 | tf_op jit(solution)/shard_map/reduce_scatter | solution.py:276
  425.5 13.8 %copy-start.45 = (s32[985,2]{0,1:T(2,128)S(1)}, s32[985,2]{0,1:T(2,128)}, u32[]{:S(2)}) copy-start(s32[985,2]{0,1:T(2,128)} %param.33) | copy-start | bytes 23644
  425.5 13.8 %copy-start.35 = (f32[985,8]{0,1:T(8,128)S(1)}, f32[985,8]{0,1:T(8,128)}, u32[]{:S(2)}) copy-start(f32[985,8]{0,1:T(8,128)} %copy-done.34) | copy-start | bytes 94564
  425.5 13.8 %copy-start.54 = (f32[985]{0:T(1024)S(1)}, f32[985]{0:T(1024)}, u32[]{:S(2)}) copy-start(f32[985]{0:T(1024)} %copy-done.53) | copy-start | bytes 11824
  425.5 13.8 %copy-start.58 = (f32[985]{0:T(1024)S(1)}, f32[985]{0:T(1024)}, u32[]{:S(2)}) copy-start(f32[985]{0:T(1024)} %copy-done.57) | copy-start | bytes 11824
  503.6 14.0 %slice-start = ((s8[8192000]{0:T(1024)(128)(4,1)}), s8[4194304]{0:T(1024)(128)(4,1)S(1)}, s32[]{:S(2)}) async-start(s8[8192000]{0:T(1024)(128)(4,1)} %bitcast.110), calls=%async_computation.22 | async-start | bytes 8388608
  520.5 94.3 %reduce-scatter.14.cloned.1.call-start = ((), (), s32[]{:S(2)}) async-start(), calls=%async_computation.14 | async-start | bytes 1966080 | tf_op jit(solution)/shard_map/reduce_scatter | solution.py:267
  555.3 46.7 %copy-start.62 = (f32[4,1,128]{2,1,0:T(1,128)S(1)}, f32[4,1,128]{2,1,0:T(1,128)}, u32[]{:S(2)}) copy-start(f32[4,1,128]{2,1,0:T(1,128)} %copy-done.61) | copy-start | bytes 6148
  555.3 76.4 %reduce-scatter.22.cloned.1.call-start = ((), (), s32[]{:S(2)}) async-start(), calls=%async_computation.18 | async-start | bytes 163840
  610.9 97.3 %all-reduce.13.cloned.1.call-start = ((), (), s32[]{:S(2)}) async-start(), calls=%async_computation.21 | async-start | bytes 1048576 | tf_op jit(solution)/shard_map/psum | solution.py:295
  (45 other events, 224.4 us)
Sparse Core Ops, SparseCore 0:
  9.7 22.3 all-gather.10
  130.0 24.0 all-gather.12
  155.6 22.5 all-gather.14
  304.9 21.0 reduce-scatter.25
  338.2 23.0 reduce-scatter.23
  397.3 32.7 reduce-scatter.19
  432.8 31.4 reduce-scatter.17
  520.6 20.7 reduce-scatter.15
  555.4 27.4 reduce-scatter.13
  611.0 20.5 reduce-scatter.21
  635.5 72.6 all-reduce.12
where the time goes:
time: 726 us; the launch traced here: 719 us
  matrix products  204 us (28%)
  local copies, waits for them, and re-layouts  138 us (19%)
  waiting for transfers between devices  136 us (19%)
  blocking collectives  126 us (17%)
  other arithmetic  76 us (10%)
  starting transfers between devices  22.2 us (3%)
  between operations  16.1 us (2%)
    dot_general x1, matrix products, shards(): jnp.dot(flat_in, first_weight, preferred_element_type=jnp.float32)  70.8 us
    psum x1, waiting for transfers between devices, shards(): lax.psum(shares[2].astype(jnp.bfloat16), 'expert').astype(jnp.float32)  49.8 us
    pmax x1, blocking collectives, shards(): peak_logit = lax.pmax(head_peak, ('expert', 'fsdp'))  38 us
    dot_general x1, matrix products, shards(): jnp.einsum('rd,hd->rh', flat_grad, second_weight, preferred_element_type=...  31.9 us
    all_to_all x1, waiting for transfers between devices, shards(): lax.all_to_all(produced, 'expert', split_axis=0, concat_axis=0, tiled=True)  28.8 us
    all_to_all x1, waiting for transfers between devices, shards(): lax.all_to_all(outgoing, 'expert', split_axis=0, concat_axis=0, tiled=True)  27.6 us
    all_to_all x1, waiting for transfers between devices, shards(): lax.all_to_all(row_grad, 'expert', split_axis=0, concat_axis=0, tiled=True)  23.3 us
    psum x1, blocking collectives, shards(): lax.psum(shares[0].astype(jnp.bfloat16), 'expert').astype(jnp.float32)  21.7 us
  transfers between devices with their start and end apart: 15, of which 5 were waited for; matrix products, arithmetic and copies ran while one was open for 49% of the time, Pallas kernels for 0%

commit v1 on v0

--- a/solution.py
+++ b/solution.py
@@ -6,6 +6,18 @@
 HEADS = 8
 norm_eps = 1e-06
 highest = lax.Precision.HIGHEST
+
+
+def rotated_exchange(shard, axis, split, join):
+    ways, here = (lax.axis_size(axis), lax.axis_index(axis))
+    width = shard.shape[split] // ways
+    turned = jnp.roll(shard, -here * width, axis=split)
+    got = [lax.slice_in_dim(turned, 0, width, axis=split)]
+    for far in range(1, ways):
+        sent = lax.slice_in_dim(turned, far * width, (far + 1) * width, axis=split)
+        got.append(lax.ppermute(sent, axis, [(d, (d + far) % ways) for d in range(ways)]))
+    line = jnp.concatenate(got[::-1], axis=join)
+    return jnp.roll(line, (here + 1) * got[0].shape[join], axis=join)
 
 
 def layer_norm(matrix, norm_gain, norm_shift):
@@ -138,7 +150,7 @@
         .set(slot_rows)
         .reshape(expert_total, capacity, feature_width)
     )
-    arrived = lax.all_to_all(outgoing, "expert", split_axis=0, concat_axis=0, tiled=True)
+    arrived = rotated_exchange(outgoing, "expert", 0, 0)
     flat_in = arrived.reshape(-1, feature_width)
     activation = gelu_exact(
         jnp.dot(flat_in, first_weight, preferred_element_type=jnp.float32) + first_bias

time: 726 us -> 807 us (1.11)
  waiting for transfers between devices: 136 us -> 182 us
  starting transfers between devices: 22.2 us -> 42.9 us
  local copies, waits for them, and re-layouts: 138 us -> 154 us
    ppermute x0 -> x7, waiting for transfers between devices: none -> 97.6 us  [rotated_exchange(): lax.ppermute(sent, axis, [(d, (d + far) % ways) for d in range(ways)])]
    ppermute x0 -> x7, starting transfers between devices: none -> 29 us  [rotated_exchange(): lax.ppermute(sent, axis, [(d, (d + far) % ways) for d in range(ways)])]
    all_to_all x1 -> x0, waiting for transfers between devices: 27.6 us -> none  [shards(): lax.all_to_all(outgoing, 'expert', split_axis=0, concat_axis=0, tiled=True)]
    psum x1, waiting for transfers between devices: 49.8 us -> 38.5 us  [shards(): lax.psum(shares[2].astype(jnp.bfloat16), 'expert').astype(jnp.float32)]
    unnamed x175 -> x182, local copies, waits for them, and re-layouts: 15.2 us -> 25.1 us
    all_to_all x1, waiting for transfers between devices: 23.3 us -> 13.6 us  [shards(): lax.all_to_all(row_grad, 'expert', split_axis=0, concat_axis=0, tiled=True)]
  transfers between devices with their start and end apart: 15 -> 21, of which waited for: 5 -> 5; matrix products, arithmetic and copies ran while one was open for 49% -> 52% of each run, Pallas kernels for 0% -> 0%
where the time goes in v1:
time: 807 us; the launch traced here: 801 us
  matrix products  198 us (25%)
  waiting for transfers between devices  182 us (23%)
  local copies, waits for them, and re-layouts  154 us (19%)
  blocking collectives  126 us (16%)
  other arithmetic  82.9 us (10%)
  starting transfers between devices  42.9 us (5%)
  between operations  15.9 us (2%)
    ppermute x7, waiting for transfers between devices, rotated_exchange(): lax.ppermute(sent, axis, [(d, (d + far) % ways) for d in range(ways)])  97.6 us
    dot_general x1, matrix products, shards(): jnp.dot(flat_in, first_weight, preferred_element_type=jnp.float32)  68 us
    psum x1, waiting for transfers between devices, shards(): lax.psum(shares[2].astype(jnp.bfloat16), 'expert').astype(jnp.float32)  38.5 us
    pmax x1, blocking collectives, shards(): peak_logit = lax.pmax(head_peak, ('expert', 'fsdp'))  37.2 us
    dot_general x1, matrix products, shards(): jnp.einsum('rd,hd->rh', flat_grad, second_weight, preferred_element_type=...  32 us
    all_to_all x1, waiting for transfers between devices, shards(): lax.all_to_all(produced, 'expert', split_axis=0, concat_axis=0, tiled=True)  29.6 us
    ppermute x7, starting transfers between devices, rotated_exchange(): lax.ppermute(sent, axis, [(d, (d + far) % ways) for d in range(ways)])  29 us
    unnamed x182, local copies, waits for them, and re-layouts  25.1 us
  transfers between devices with their start and end apart: 21, of which 5 were waited for; matrix products, arithmetic and copies ran while one was open for 52% of the time, Pallas kernels for 0%

profile of v1, /device:TPU:0, one launch (start us, length us, event | category | flops | bytes accessed | tf_op | source)
XLA Modules:
  0.0 801.0 jit_solution(8937736740194227322)
XLA Ops:
  14.2 6.0 all-gather
  20.2 5.3 all-gather.1
  25.5 5.0 all-gather.3
  30.6 5.0 all-gather.2
  35.6 5.0 all-gather.4
  40.6 5.0 all-gather.5
  45.7 5.0 all-gather.6
  50.7 5.0 all_gather.55
  56.3 5.1 all_gather.51
  61.5 5.1 all_gather.53
  72.8 10.3 %all_gather.47 = bf16[512,512]{1,0:T(8,128)(2,1)} all-gather(bf16[128,512]{1,0:T(8,128)(2,1)S(1)} %copy-done.45), channel_id=1, replica_groups=mesh['expert'=8,'fsdp'=4] {'fsdp'}, dimensions={0}, use_global_device_ids=true | all-gather | bytes 655360 | tf_op jit(solution)/shard_map/all_gather | solution.py:70
  85.9 4.9 mul.251
  90.7 5.9 mul.252
  104.9 4.0 copy.109
  114.4 4.1 reshape.279
  118.5 4.4 copy.111
  145.5 13.4 %scatter_custom_fusion = bf16[3456,512]{1,0:T(8,128)(2,1)} fusion(s32[1970]{0:T(1024)S(1)} %bitcast.138, bf16[1970,512]{1,0:T(8,128)(2,1)} %reshape.330, bf16[]{:T(256)} %constant.33.clone.1), kind=kCustom, calls=%fused_computation.75 | custom fusion | bytes 3539456 | tf_op jit(solution)/shard_map/scatter | solution.py:150
  174.5 18.4 %scatter_custom_fusion.1 = bf16[3456,512]{1,0:T(8,128)(2,1)} fusion(s32[1970]{0:T(1024)} %bitcast.139, f32[1970,512]{1,0:T(8,128)} %mul.252, f32[1970]{0:T(1024)S(1)} %mul.249, bf16[]{:T(256)} %constant.33.clone.1), kind=kCustom, calls=%fused_computation.69 | custom fusion | flops 2017280 | bytes 7594184 | tf_op jit(solution)/shard_map/scatter | solution.py:183
  193.0 4.5 all-to-all-start.1
  199.4 19.1 %collective-permute-start.4 = (bf16[1,432,512]{2,1,0:T(8,128)(2,1)}, bf16[1,432,512]{2,1,0:T(8,128)(2,1)S(1)}, u32[]{:S(2)}, u32[]{:S(2)}) collective-permute-start(bf16[1,432,512]{2,1,0:T(8,128)(2,1)} %get-tuple-element.55), channel_id=1, source_target_pairs={{0,12},{4,16},{8,20},{12,24},{16,28},{20,0},{24,4},{28,8},{1,13},{... | collective-permute-start | bytes 1327112 | tf_op jit(solution)/shard_map/ppermute | solution.py:18
  221.9 14.0 %collective-permute-done.3 = bf16[1,432,512]{2,1,0:T(8,128)(2,1)} collective-permute-done((bf16[1,432,512]{2,1,0:T(8,128)(2,1)}, bf16[1,432,512]{2,1,0:T(8,128)(2,1)}, u32[]{:S(2)}, u32[]{:S(2)}) %collective-permute-start.3) | collective-permute-done | bytes 442400 | tf_op jit(solution)/shard_map/ppermute | solution.py:18
  237.0 83.6 %collective-permute-done.4 = bf16[1,432,512]{2,1,0:T(8,128)(2,1)S(1)} collective-permute-done((bf16[1,432,512]{2,1,0:T(8,128)(2,1)}, bf16[1,432,512]{2,1,0:T(8,128)(2,1)S(1)}, u32[]{:S(2)}, u32[]{:S(2)}) %collective-permute-start.4) | collective-permute-done | bytes 442400 | tf_op jit(solution)/shard_map/ppermute | solution.py:18
  322.1 68.0 %multiply_convert_fusion = (bf16[3456,2048]{1,0:T(8,128)(2,1)}, f32[3456,2048]{1,0:T(8,128)}, f32[3456,2048]{1,0:T(8,128)}) fusion(f32[2048]{0:T(1024)S(1)} %bitcast.148, bf16[3456,512]{1,0:T(8,128)(2,1)S(1)} %bitcast.118, bf16[1,512,2048]{2,1,0:T(8,128)(2,1)} %all-gather.13.cloned.1.call-done), kind=kOutput, calls=%fused_computation.7 | convolution fusion | flops 7714897920 | bytes 76423168 | tf_op jit(solution)/shard_map/dot_general | solution.py:156
  390.1 12.5 %add_convert_fusion.1 = bf16[3456,512]{1,0:T(8,128)(2,1)} fusion(bf16[3456,2048]{1,0:T(8,128)(2,1)} %get-tuple-element.49, f32[512]{0:T(512)S(1)} %bitcast.150, bf16[1,2048,512]{2,1,0:T(8,128)(2,1)} %all-gather.15.cloned.1.call-done), kind=kOutput, calls=%fused_computation.29 | convolution fusion | flops 7251296256 | bytes 19793920 | tf_op jit(solution)/shard_map/dot_general | solution.py:159
  402.6 4.5 all-to-all-start
  411.0 32.0 %fusion.53 = (bf16[2048]{0:T(1024)(128)(2,1)S(1)}, bf16[3456,2048]{1,0:T(8,128)(2,1)}) fusion(f32[3456,2048]{1,0:T(8,128)} %get-tuple-element.50, bf16[3456,512]{1,0:T(8,128)(2,1)} %bitcast.27, bf16[1,2048,512]{2,1,0:T(8,128)(2,1)} %all-gather.15.cloned.1.call-done, f32[3456,2048]{1,0:T(8,128)} %get-tuple-element.65, f32[2048]{0:T(1024)S(1)} %bitcast.149), kind=kOutput, calls=%fused_computation.153 | convolution fusion | flops 7361001472 | bytes 76427264 | tf_op jit(solution)/shard_map/rd,hd->rh/dot_general | solution.py:196
  444.2 12.7 %convolution_convert_fusion = bf16[3456,512]{1,0:T(8,128)(2,1)} fusion(bf16[3456,2048]{1,0:T(8,128)(2,1)} %get-tuple-element.76, bf16[1,512,2048]{2,1,0:T(8,128)(2,1)} %all-gather.13.cloned.1.call-done), kind=kOutput, calls=%fused_computation.32 | convolution fusion | flops 7249526784 | bytes 19791872 | tf_op jit(solution)/shard_map/rh,dh->rd/dot_general | solution.py:201
  456.8 29.6 %all-to-all-done = bf16[8,432,512]{2,1,0:T(8,128)(2,1)S(1)} async-done(((bf16[8,432,512]{2,1,0:T(8,128)(2,1)}), bf16[8,432,512]{2,1,0:T(8,128)(2,1)S(1)}, u32[]{:S(2)}, u32[]{:S(2)}) %all-to-all-start) | async-done | bytes 3538976 | tf_op jit(solution)/shard_map/all_to_all | solution.py:162
  492.1 11.6 %gather_fusion = bf16[1970,512]{1,0:T(8,128)(2,1)} fusion(bf16[3456,512]{1,0:T(8,128)(2,1)} %bitcast.115, s32[2048]{0:T(1024)S(1)} %copy-done.50), kind=kCustom, calls=%fused_computation | custom fusion | bytes 4042440 | tf_op jit(solution)/shard_map/gather | solution.py:164
  503.7 5.5 reshape.306
  509.2 13.9 %multiply_reduce_fusion.3 = (f32[985,2]{1,0:T(8,128)}, f32[985,512]{1,0:T(8,128)}) fusion(f32[985,2,512]{2,1,0:T(2,128)} %reshape.306, f32[985,512]{1,0:T(8,128)} %reshape.308, f32[985,2]{1,0:T(8,128)} %copy.114), kind=kLoop, calls=%fused_computation.35 | loop fusion | flops 3528270 | bytes 8084880 | tf_op jit(solution)/shard_map/reduce_sum | solution.py:174
  531.1 13.1 %fusion.9 = bf16[1,2048,512]{2,1,0:T(8,128)(2,1)} fusion(bf16[3456,2048]{1,0:T(8,128)(2,1)} %get-tuple-element.49, bf16[3456,512]{1,0:T(8,128)(2,1)} %bitcast.27), kind=kOutput, calls=%fused_computation.42 | convolution fusion | flops 7248805888 | bytes 19791872 | tf_op jit(solution)/shard_map/rh,rd->hd/dot_general | solution.py:194
  544.2 13.0 %fusion.10 = bf16[1,512,2048]{2,1,0:T(8,128)(2,1)} fusion(bf16[3456,512]{1,0:T(8,128)(2,1)} %bitcast.119, bf16[3456,2048]{1,0:T(8,128)(2,1)} %get-tuple-element.76), kind=kOutput, calls=%fused_computation.43 | convolution fusion | flops 7248805888 | bytes 19791872 | tf_op jit(solution)/shard_map/rd,rh->dh/dot_general | solution.py:198
  557.5 13.6 %all-to-all-done.2 = bf16[8,432,512]{2,1,0:T(8,128)(2,1)S(1)} async-done(((bf16[8,432,512]{2,1,0:T(8,128)(2,1)}), bf16[8,432,512]{2,1,0:T(8,128)(2,1)S(1)}, u32[]{:S(2)}, u32[]{:S(2)}) %all-to-all-start.2) | async-done | bytes 3538976 | tf_op jit(solution)/shard_map/all_to_all | solution.py:205
  571.2 9.2 %gather_fusion.1 = bf16[1970,512]{1,0:T(8,128)(2,1)} fusion(bf16[3456,512]{1,0:T(8,128)(2,1)S(1)} %bitcast.114, s32[2048]{0:T(1024)S(1)} %copy-done.51), kind=kCustom, calls=%fused_computation.1 | custom fusion | bytes 4042440 | tf_op jit(solution)/shard_map/gather | solution.py:207
  580.4 5.5 reshape.309
  585.9 8.4 %reduce_sum.274 = f32[985,512]{1,0:T(8,128)} reduce(f32[985,2,512]{2,1,0:T(2,128)} %reshape.309, f32[]{:T(128)} %constant.51.clone.1), dimensions={1}, to_apply=%region_15.17 | reduce | flops 504320 | bytes 6051844 | tf_op jit(solution)/shard_map/reduce_sum | solution.py:213
  594.3 4.7 multiply_reduce_fusion.6
  604.4 4.5 copy.119
  611.7 6.7 multiply_reduce_fusion.1
  618.4 4.7 multiply_convert_fusion.1
  633.8 4.1 copy.129
  651.2 4.0 reshape.298
  672.4 37.2 %pmax.7 = f32[8]{0:T(128)S(1)} all-reduce(f32[8]{0:T(128)S(1)} %get-tuple-element.18), channel_id=1, replica_groups=mesh['expert'=8,'fsdp'=4] {'expert','fsdp'}, use_global_device_ids=true, to_apply=%region_58.60 | all-reduce | flops 8 | bytes 64 | tf_op jit(solution)/shard_map/pmax | solution.py:330
  709.8 4.8 multiply_reduce_fusion.7
  718.2 6.4 all-reduce.10
  725.2 20.5 %all-reduce.8 = (bf16[128]{0:T(256)(128)(2,1)S(1)}, bf16[128]{0:T(256)(128)(2,1)S(1)}, bf16[128]{0:T(256)(128)(2,1)S(1)}, bf16[128]{0:T(256)(128)(2,1)S(1)}, bf1...) all-reduce(bf16[128]{0:T(256)(128)(2,1)S(1)} %dynamic-slice.1, ...), channel_id=1, replica_groups=mesh['expert'=8,'fsdp'=4] {'expert'}, use_global_device_ids=true, to_apply=%region_26.28 | all-reduce | flops 1920 | bytes 7680 | tf_op jit(solution)/shard_map/psum | solution.py:305
  752.2 38.5 %all-reduce.13.cloned.1.call-done = (bf16[128,1536]{1,0:T(8,128)(2,1)}, bf16[128,512]{1,0:T(8,128)(2,1)}) async-done(((bf16[128,1536]{1,0:T(8,128)(2,1)}, bf16[128,512]{1,0:T(8,128)(2,1)}), (bf16[128,1536]{1,0:T(8,128)(2,1)}, bf16[128,512]{1,0:T(8,128)(2,1)})) %all-reduce.13.cloned.1.call-update) | async-done | bytes 524304 | tf_op jit(solution)/shard_map/psum | solution.py:307
  (333 shorter events, 157.4 us)
Async XLA Ops:
  7.2 18.3 %copy-start.68 = (bf16[128]{0:T(256)(128)(2,1)S(1)}, bf16[128]{0:T(256)(128)(2,1)}, u32[]{:S(2)}) copy-start(bf16[128]{0:T(256)(128)(2,1)} %param.24) | copy-start | bytes 772
  7.2 23.3 %copy-start.69 = (bf16[128]{0:T(256)(128)(2,1)S(1)}, bf16[128]{0:T(256)(128)(2,1)}, u32[]{:S(2)}) copy-start(bf16[128]{0:T(256)(128)(2,1)} %param.25) | copy-start | bytes 772
  7.3 28.3 %copy-start.70 = (bf16[128]{0:T(256)(128)(2,1)S(1)}, bf16[128]{0:T(256)(128)(2,1)}, u32[]{:S(2)}) copy-start(bf16[128]{0:T(256)(128)(2,1)} %param.27) | copy-start | bytes 772
  7.3 33.4 %copy-start.71 = (bf16[128]{0:T(256)(128)(2,1)S(1)}, bf16[128]{0:T(256)(128)(2,1)}, u32[]{:S(2)}) copy-start(bf16[128]{0:T(256)(128)(2,1)} %param.28) | copy-start | bytes 772
  7.3 38.4 %copy-start.72 = (bf16[128]{0:T(256)(128)(2,1)S(1)}, bf16[128]{0:T(256)(128)(2,1)}, u32[]{:S(2)}) copy-start(bf16[128]{0:T(256)(128)(2,1)} %param.29) | copy-start | bytes 772
  7.3 43.4 %copy-start.73 = (bf16[1,128]{1,0:T(2,128)(2,1)S(1)}, bf16[1,128]{1,0:T(2,128)(2,1)}, u32[]{:S(2)}) copy-start(bf16[1,128]{1,0:T(2,128)(2,1)} %param.34) | copy-start | bytes 772
  7.3 49.0 %copy-start.63 = (bf16[128,8]{0,1:T(8,128)(2,1)S(1)}, bf16[128,8]{0,1:T(8,128)(2,1)}, u32[]{:S(2)}) copy-start(bf16[128,8]{0,1:T(8,128)(2,1)} %param.30) | copy-start | bytes 6148
  7.3 54.2 %copy-start.64 = (bf16[1,512]{1,0:T(2,128)(2,1)S(1)}, bf16[1,512]{1,0:T(2,128)(2,1)}, u32[]{:S(2)}) copy-start(bf16[1,512]{1,0:T(2,128)(2,1)} %param.32) | copy-start | bytes 3076
  7.3 89.3 %all-gather.11.cloned.1.call-start = ((), (), s32[]{:S(2)}) async-start(), calls=%async_computation.10 | async-start | bytes 1966080 | tf_op jit(solution)/shard_map/all_gather | solution.py:67
  8.1 314.0 %all-gather.13.cloned.1.call-start = ((), (), s32[]{:S(2)}) async-start(), calls=%async_computation.11 | async-start | bytes 2621440 | tf_op jit(solution)/shard_map/all_gather | solution.py:75
  8.8 381.3 %all-gather.15.cloned.1.call-start = ((), (), s32[]{:S(2)}) async-start(), calls=%async_computation.12 | async-start | bytes 2621440 | tf_op jit(solution)/shard_map/all_gather | solution.py:77
  11.1 85.5 %copy-start.39 = (f32[985]{0:T(1024)}, f32[985]{0:T(1024)S(1)}, u32[]{:S(2)}) copy-start(f32[985]{0:T(1024)S(1)} %div.38) | copy-start | bytes 11824
  11.1 61.6 %copy-start.45 = (bf16[128,512]{1,0:T(8,128)(2,1)S(1)}, bf16[128,512]{1,0:T(8,128)(2,1)}, u32[]{:S(2)}) copy-start(bf16[128,512]{1,0:T(8,128)(2,1)} %param.26) | copy-start | bytes 393220
  14.2 122.7 %copy-start.5 = (f32[985,512]{1,0:T(8,128)}, f32[985,512]{1,0:T(8,128)S(1)}, u32[]{:S(2)}) copy-start(f32[985,512]{1,0:T(8,128)S(1)} %reshape.278) | copy-start | bytes 6051844
  20.2 76.5 %copy-start.46 = (f32[4,1,128]{2,1,0:T(1,128)}, f32[4,1,128]{2,1,0:T(1,128)S(1)}, u32[]{:S(2)}) copy-start(f32[4,1,128]{2,1,0:T(1,128)S(1)} %convert_element_type.334) | copy-start | bytes 6148
  25.5 71.1 %copy-start.55 = (f32[4,1,128]{2,1,0:T(1,128)}, f32[4,1,128]{2,1,0:T(1,128)S(1)}, u32[]{:S(2)}) copy-start(f32[4,1,128]{2,1,0:T(1,128)S(1)} %convert_element_type.335) | copy-start | bytes 6148
  45.7 94.3 %copy-start.52 = (f32[4,1,128]{2,1,0:T(1,128)}, f32[4,1,128]{2,1,0:T(1,128)S(1)}, u32[]{:S(2)}) copy-start(f32[4,1,128]{2,1,0:T(1,128)S(1)} %convert_element_type.339) | copy-start | bytes 6148
  50.7 89.3 %copy-start.61 = (f32[4,1,128]{2,1,0:T(1,128)}, f32[4,1,128]{2,1,0:T(1,128)S(1)}, u32[]{:S(2)}) copy-start(f32[4,1,128]{2,1,0:T(1,128)S(1)} %convert_element_type.340) | copy-start | bytes 6148
  61.5 78.5 %copy-start.48 = (bf16[512,8]{0,1:T(8,128)(2,1)}, bf16[512,8]{0,1:T(8,128)(2,1)S(1)}, u32[]{:S(2)}) copy-start(bf16[512,8]{0,1:T(8,128)(2,1)S(1)} %all_gather.51) | copy-start | bytes 24580
  67.3 29.3 %copy-start.41 = (f32[985]{0:T(1024)}, f32[985]{0:T(1024)S(1)}, u32[]{:S(2)}) copy-start(f32[985]{0:T(1024)S(1)} %rsqrt.20) | copy-start | bytes 11824
  72.2 73.3 %copy-start.60 = (s32[1970,1]{0,1:T(1,128)}, s32[1970,1]{0,1:T(1,128)S(1)}, u32[]{:S(2)}) copy-start(s32[1970,1]{0,1:T(1,128)S(1)} %compare_select_fusion) | copy-start | bytes 23644
  142.4 26.7 %copy-start.54 = (f32[985]{0:T(1024)}, f32[985]{0:T(1024)S(1)}, u32[]{:S(2)}) copy-start(f32[985]{0:T(1024)S(1)} %get-tuple-element.66) | copy-start | bytes 11824
  163.8 57.0 %collective-permute-start.2 = (bf16[1,432,512]{2,1,0:T(8,128)(2,1)}, bf16[1,432,512]{2,1,0:T(8,128)(2,1)}, u32[]{:S(2)}, u32[]{:S(2)}) collective-permute-start(bf16[1,432,512]{2,1,0:T(8,128)(2,1)} %get-tuple-element.57), channel_id=1, source_target_pairs={{0,20},{4,24},{8,28},{12,0},{16,4},{20,8},{24,12},{28,16},{1,21},{... | collective-permute-start | bytes 1327112 | tf_op jit(solution)/shard_map/ppermute | solution.py:18
  167.2 52.4 %collective-permute-start.1 = (bf16[1,432,512]{2,1,0:T(8,128)(2,1)}, bf16[1,432,512]{2,1,0:T(8,128)(2,1)}, u32[]{:S(2)}, u32[]{:S(2)}) collective-permute-start(bf16[1,432,512]{2,1,0:T(8,128)(2,1)} %get-tuple-element.58), channel_id=1, source_target_pairs={{0,24},{4,28},{8,0},{12,4},{16,8},{20,12},{24,16},{28,20},{1,25},{... | collective-permute-start | bytes 1327112 | tf_op jit(solution)/shard_map/ppermute | solution.py:18
  168.6 30.8 %collective-permute-start = (bf16[1,432,512]{2,1,0:T(8,128)(2,1)}, bf16[1,432,512]{2,1,0:T(8,128)(2,1)}, u32[]{:S(2)}, u32[]{:S(2)}) collective-permute-start(bf16[1,432,512]{2,1,0:T(8,128)(2,1)} %get-tuple-element.59), channel_id=1, source_target_pairs={{0,28},{4,0},{8,4},{12,8},{16,12},{20,16},{24,20},{28,24},{1,29},{... | collective-permute-start | bytes 1327112 | tf_op jit(solution)/shard_map/ppermute | solution.py:18
  169.7 66.2 %collective-permute-start.3 = (bf16[1,432,512]{2,1,0:T(8,128)(2,1)}, bf16[1,432,512]{2,1,0:T(8,128)(2,1)}, u32[]{:S(2)}, u32[]{:S(2)}) collective-permute-start(bf16[1,432,512]{2,1,0:T(8,128)(2,1)} %get-tuple-element.56), channel_id=1, source_target_pairs={{0,16},{4,20},{8,24},{12,28},{16,0},{20,4},{24,8},{28,12},{1,17},{... | collective-permute-start | bytes 1327112 | tf_op jit(solution)/shard_map/ppermute | solution.py:18
  193.0 209.6 %all-to-all-start.1 = ((bf16[8,432,512]{2,1,0:T(8,128)(2,1)}), bf16[8,432,512]{2,1,0:T(8,128)(2,1)}, u32[]{:S(2)}, u32[]{:S(2)}) async-start(bf16[8,432,512]{2,1,0:T(8,128)(2,1)} %bitcast.116), calls=%async_computation.1 | async-start | bytes 7077888 | tf_op jit(solution)/shard_map/all_to_all | solution.py:186
  197.5 123.2 %collective-permute-start.6 = (bf16[1,432,512]{2,1,0:T(8,128)(2,1)}, bf16[1,432,512]{2,1,0:T(8,128)(2,1)S(1)}, u32[]{:S(2)}, u32[]{:S(2)}) collective-permute-start(bf16[1,432,512]{2,1,0:T(8,128)(2,1)} %get-tuple-element.53), channel_id=1, source_target_pairs={{0,4},{4,8},{8,12},{12,16},{16,20},{20,24},{24,28},{28,0},{1,5},{5... | collective-permute-start | bytes 1327112 | tf_op jit(solution)/shard_map/ppermute | solution.py:18
  199.4 121.2 %collective-permute-start.4 = (bf16[1,432,512]{2,1,0:T(8,128)(2,1)}, bf16[1,432,512]{2,1,0:T(8,128)(2,1)S(1)}, u32[]{:S(2)}, u32[]{:S(2)}) collective-permute-start(bf16[1,432,512]{2,1,0:T(8,128)(2,1)} %get-tuple-element.55), channel_id=1, source_target_pairs={{0,12},{4,16},{8,20},{12,24},{16,28},{20,0},{24,4},{28,8},{1,13},{... | collective-permute-start | bytes 1327112 | tf_op jit(solution)/shard_map/ppermute | solution.py:18
  219.5 101.1 %collective-permute-start.5 = (bf16[1,432,512]{2,1,0:T(8,128)(2,1)}, bf16[1,432,512]{2,1,0:T(8,128)(2,1)S(1)}, u32[]{:S(2)}, u32[]{:S(2)}) collective-permute-start(bf16[1,432,512]{2,1,0:T(8,128)(2,1)} %get-tuple-element.54), channel_id=1, source_target_pairs={{0,8},{4,12},{8,16},{12,20},{16,24},{20,28},{24,0},{28,4},{1,9},{5... | collective-permute-start | bytes 1327112 | tf_op jit(solution)/shard_map/ppermute | solution.py:18
  322.0 68.0 %copy-start.26 = (bf16[8,432,512]{2,1,0:T(8,128)(2,1)}, bf16[8,432,512]{2,1,0:T(8,128)(2,1)S(1)}, u32[]{:S(2)}) copy-start(bf16[8,432,512]{2,1,0:T(8,128)(2,1)S(1)} %fusion.7) | copy-start | bytes 10616836
  322.1 68.0 %copy-start.65 = (f32[1,512]{1,0:T(1,128)S(1)}, f32[1,512]{1,0:T(1,128)}, u32[]{:S(2)}) copy-start(f32[1,512]{1,0:T(1,128)} %add.224) | copy-start | bytes 6148
  402.6 83.8 %all-to-all-start = ((bf16[8,432,512]{2,1,0:T(8,128)(2,1)}), bf16[8,432,512]{2,1,0:T(8,128)(2,1)S(1)}, u32[]{:S(2)}, u32[]{:S(2)}) async-start(bf16[8,432,512]{2,1,0:T(8,128)(2,1)} %bitcast.121), calls=%async_computation | async-start | bytes 7077888 | tf_op jit(solution)/shard_map/all_to_all | solution.py:162
  407.2 257.0 %reduce-scatter.26.cloned.1.call-start = ((), (), s32[]{:S(2)}) async-start(), calls=%async_computation.19 | async-start | bytes 163840
  410.6 255.0 %reduce-scatter.24.cloned.1.call-start = ((), (), s32[]{:S(2)}) async-start(), calls=%async_computation.18 | async-start | bytes 655360
  488.2 83.0 %all-to-all-start.2 = ((bf16[8,432,512]{2,1,0:T(8,128)(2,1)}), bf16[8,432,512]{2,1,0:T(8,128)(2,1)S(1)}, u32[]{:S(2)}, u32[]{:S(2)}) async-start(bf16[8,432,512]{2,1,0:T(8,128)(2,1)} %bitcast.120), calls=%async_computation.2 | async-start | bytes 7077888 | tf_op jit(solution)/shard_map/all_to_all | solution.py:205
  491.9 175.3 %reduce-scatter.22.cloned.1.call-start = ((), (), s32[]{:S(2)}) async-start(), calls=%async_computation.17 | async-start | bytes 163840
  509.2 17.8 %copy-start.36 = (f32[985]{0:T(1024)S(1)}, f32[985]{0:T(1024)}, u32[]{:S(2)}) copy-start(f32[985]{0:T(1024)} %copy-done.35) | copy-start | bytes 11824
  509.2 17.8 %copy-start.38 = (f32[985]{0:T(1024)S(1)}, f32[985]{0:T(1024)}, u32[]{:S(2)}) copy-start(f32[985]{0:T(1024)} %copy-done.37) | copy-start | bytes 11824
  531.0 137.0 %reduce-scatter.20.cloned.1.call-start = ((), (), s32[]{:S(2)}) async-start(), calls=%async_computation.16 | async-start | bytes 2621440 | tf_op jit(solution)/shard_map/reduce_scatter | solution.py:323
  544.2 27.0 %copy-start.51 = (s32[2048]{0:T(1024)S(1)}, s32[2048]{0:T(1024)}, u32[]{:S(2)}) copy-start(s32[2048]{0:T(1024)} %pad_clamp_fusion) | copy-start | bytes 24580
  544.2 126.1 %reduce-scatter.18.cloned.1.call-start = ((), (), s32[]{:S(2)}) async-start(), calls=%async_computation.15 | async-start | bytes 2621440 | tf_op jit(solution)/shard_map/reduce_scatter | solution.py:317
  557.3 159.5 %reduce-scatter.16.cloned.1.call-start = ((), (), s32[]{:S(2)}) async-start(), calls=%async_computation.14 | async-start | bytes 655360 | tf_op jit(solution)/shard_map/reduce_scatter | solution.py:288
  630.5 86.2 %reduce-scatter.14.cloned.1.call-start = ((), (), s32[]{:S(2)}) async-start(), calls=%async_computation.13 | async-start | bytes 1966080 | tf_op jit(solution)/shard_map/reduce_scatter | solution.py:279
  662.8 46.8 %copy-start.74 = (s32[8]{0:T(128)S(1)}, s32[8]{0:T(128)}, u32[]{:S(2)}) copy-start(s32[8]{0:T(128)} %param.36) | copy-start | bytes 100
  662.8 127.8 %all-reduce.13.cloned.1.call-start = ((), (), s32[]{:S(2)}) async-start(), calls=%async_computation.20 | async-start | bytes 1048576 | tf_op jit(solution)/shard_map/psum | solution.py:307
  716.7 33.1 %copy-start.19 = (f32[985,512]{1,0:T(8,128)S(1)}, f32[985,512]{1,0:T(8,128)}, u32[]{:S(2)}) copy-start(f32[985,512]{1,0:T(8,128)} %multiply_add_fusion) | copy-start | bytes 6051844
  716.7 34.7 %copy-start.27 = (bf16[128,1536]{1,0:T(8,128)(2,1)S(1)}, bf16[128,1536]{1,0:T(8,128)(2,1)}, u32[]{:S(2)}) copy-start(bf16[128,1536]{1,0:T(8,128)(2,1)} %param.23) | copy-start | bytes 1179652
  (51 other events, 269.7 us)
Sparse Core Ops, SparseCore 0:
  9.7 22.3 all-gather.10
  33.7 22.6 all-gather.12
  57.9 24.8 all-gather.14
  410.7 20.0 reduce-scatter.25
  444.3 22.0 reduce-scatter.23
  531.2 19.9 reduce-scatter.21
  553.9 31.3 reduce-scatter.19
  587.8 31.4 reduce-scatter.17
  630.7 19.5 reduce-scatter.15
  663.0 26.2 reduce-scatter.13
  716.9 73.7 all-reduce.12
